TPU v7x, 32 devices: a whole 2x2x4 slice. The times are simulated.
32 devices in a mesh: seq: 8 (over y, x, core), head: 4 (over z).
Axes of the slice: x: 2, y: 2, z: 4, core: 2. Of those that a mesh axis runs over, the one named last changes fastest.
Arguments:
- inputs: bfloat16 [4096, 4096], P('seq'), may hold values from -6 to 6
- queries: bfloat16 [4096, 4096], P('seq', 'head'), may hold values from -6 to 6
- keys: bfloat16 [4096, 4096], P('seq', 'head'), may hold values from -6 to 6
- values: bfloat16 [4096, 4096], P('seq', 'head'), may hold values from -6 to 6
- out_grad: bfloat16 [4096, 4096], P('seq', 'head'), may hold values from -6 to 6
- value_weight: bfloat16 [4096, 4096], P('seq', 'head'), may hold values from -0.125 to 0.125
Outputs:
- grad_input: bfloat16 [4096, 4096], P('seq', 'head')
- grad_query: bfloat16 [4096, 4096], P('seq', 'head')
- grad_key: bfloat16 [4096, 4096], P('seq', 'head')
- grad_value: bfloat16 [4096, 4096], P('seq', 'head')
- grad_weight: float32 [4096, 4096], P('seq', 'head')
All inputs are finite; a program needn't handle non-finite values.
Results may differ from a plain program's by a relative error of at most 0.015.
Values may be sent and summed in bfloat16 or wider, within the bound.
A program may use at most 128 MiB of HBM per device.

v0:
```python
import math

import jax
import jax.numpy as jnp
from jax import lax
from jax.sharding import PartitionSpec as P


HEAD_DIM = 128


def exchange(x, axis, bit):
    return lax.ppermute(x, axis, [(i, i ^ bit) for i in range(lax.axis_size(axis))])


def bits_of(axis):
    count = lax.axis_size(axis)
    assert count & (count - 1) == 0
    return [1 << k for k in range(count.bit_length() - 1)]


def carried_in(state, axis, later):
    here = lax.axis_index(axis)
    carried, total = jnp.zeros_like(state), state
    for bit in bits_of(axis):
        got = exchange(total.astype(jnp.bfloat16), axis, bit).astype(state.dtype)
        upper = (here & bit) != 0
        carried = carried + jnp.where(upper != later, got, 0.0)
        total = total + got
    return carried


def halving(terms, axis, bits):
    terms = dict(terms)
    for at, bit in enumerate(bits):
        leaving = [m for m in terms if m & bit]
        ahead = sum(bits[at + 1 :])
        for m in sorted(leaving, key=lambda m: -bin(m & ahead).count("1")):
            got = exchange(terms.pop(m).astype(jnp.bfloat16), axis, bit)
            terms[m ^ bit] = terms[m ^ bit].astype(jnp.float32) + got.astype(jnp.float32)
    return terms[0]


def spread(block, axis):
    first_bit, *rest = bits_of(axis)
    half = block.shape[0] // 2
    found = {0: (block[:half], block[half:])}
    whole = {0: block}
    for m in sorted(range(2, lax.axis_size(axis), 2), key=lambda m: (bin(m).count("1"), m)):
        low, high = m & -m, 1 << (m.bit_length() - 1)
        if low == high:
            whole[m] = exchange(block, axis, m)
            found[m] = (whole[m][:half], whole[m][half:])
        else:
            found[m] = (
                exchange(found[m ^ low][0], axis, low),
                exchange(found[m ^ high][1], axis, high),
            )
    for m in list(found):
        if m in whole:
            got = exchange(whole[m], axis, first_bit)
            found[m | first_bit] = (got[:half], got[half:])
        else:
            found[m | first_bit] = tuple(exchange(x, axis, first_bit) for x in found[m])
    return found


def local(inputs, queries, keys, values, out_grad, value_weight):
    f32 = jnp.float32
    high = lax.Precision.HIGHEST
    rows = queries.shape[0]
    width = queries.shape[1]
    nheads = width // HEAD_DIM
    first = lax.axis_index("seq") * rows
    posit = (first + jnp.arange(rows, dtype=jnp.int32)).astype(f32)
    factor = 1.0 / jnp.sqrt(HEAD_DIM * (posit + 1.0))
    q3 = queries.reshape(rows, nheads, HEAD_DIM)
    k3 = keys.reshape(rows, nheads, HEAD_DIM)
    v3 = values.reshape(rows, nheads, HEAD_DIM)
    o3 = out_grad.reshape(rows, nheads, HEAD_DIM)
    o3wide = o3.astype(f32)
    state_kv = jnp.einsum("thi,thj->hij", k3, v3, preferred_element_type=f32)
    state_qo = jnp.einsum(
        "thi,thj->hij", q3.astype(f32), o3wide * factor[:, None, None], precision=high
    )
    suffix = carried_in(state_qo, "seq", True)
    prefix = carried_in(state_kv, "seq", False)
    index = jnp.arange(rows, dtype=jnp.int32)
    lower = (index[:, None] >= index[None, :])[None]
    score_qk = (
        jnp.einsum("thd,shd->hts", q3, k3, preferred_element_type=f32) * factor[None, :, None]
    )
    score_qk = jnp.where(lower, score_qk, 0.0).astype(jnp.bfloat16)
    score_ov = (
        jnp.einsum("thd,shd->hts", o3, v3, preferred_element_type=f32) * factor[None, :, None]
    )
    score_ov = jnp.where(lower, score_ov, 0.0).astype(jnp.bfloat16)
    dq = jnp.einsum("hts,shd->thd", score_ov, k3, preferred_element_type=f32)
    dq = dq + factor[:, None, None] * jnp.einsum("thj,hij->thi", o3wide, prefix, precision=high)
    dk = jnp.einsum("hts,thd->shd", score_ov, q3, preferred_element_type=f32)
    dk = dk + jnp.einsum("shj,hij->shi", v3.astype(f32), suffix, precision=high)
    dv = jnp.einsum("hts,thd->shd", score_qk, o3, preferred_element_type=f32)
    dv = dv + jnp.einsum("shi,hij->shj", k3.astype(f32), suffix, precision=high)
    grad_query = dq.reshape(rows, width).astype(jnp.bfloat16)
    grad_key = dk.reshape(rows, width).astype(jnp.bfloat16)
    grad_value = dv.reshape(rows, width).astype(jnp.bfloat16)
    here, group = (lax.axis_index("seq"), lax.axis_index("head"))
    seqs, heads = (lax.axis_size("seq"), lax.axis_size("head"))
    found = spread(value_weight, "seq")
    weight = jnp.concatenate([x for m in range(seqs) for x in found[m]], axis=0)
    span = value_weight.shape[0]
    each = seqs // heads
    pieces = {}
    for m in range(heads):
        for j in range(each):
            at = here ^ ((group ^ m) * each + j)
            part = lax.dynamic_slice_in_dim(weight, at * span, span, 0)
            pieces[m, j] = lax.dot_general(
                grad_value, part, (((1,), (1,)), ((), ())), preferred_element_type=f32
            ).astype(jnp.bfloat16)
    leaving = [key for key in pieces if key[0] & 1]
    late_value, *ready = lax.optimization_barrier((grad_value, *[pieces[key] for key in leaving]))
    pieces.update(zip(leaving, ready))
    grad_input = jnp.concatenate(
        [
            halving({m: pieces[m, j] for m in range(heads)}, "head", bits_of("head"))
            for j in range(each)
        ],
        axis=1,
    ).astype(jnp.bfloat16)
    wscale = 1.0 / math.sqrt(rows * lax.axis_size("seq"))
    slab = inputs.shape[1] // seqs
    first_bit, *rest = bits_of("seq")
    sides = []
    for side in (first_bit, 0):
        chosen = [m for m in range(seqs) if m & first_bit == side]
        picked = jnp.concatenate(
            [lax.dynamic_slice_in_dim(inputs, (here ^ m) * slab, slab, 1) for m in chosen], axis=1
        )
        product = lax.dot_general(
            picked, late_value, (((0,), (0,)), ((), ())), preferred_element_type=f32
        )
        sides.append((product * wscale).astype(jnp.bfloat16))
    arrived = exchange(sides[0], "seq", first_bit)
    paired = sides[1].astype(f32) + arrived.astype(f32)
    half = width // 2
    outs = []
    for at, order in ((0, rest), (half, rest[::-1])):
        terms = {
            m: paired[k * slab : (k + 1) * slab, at : at + half].astype(jnp.bfloat16)
            for k, m in enumerate(chosen)
        }
        terms = {m: lax.optimization_barrier(x) if m else x for m, x in terms.items()}
        outs.append(halving(terms, "seq", order))
    grad_weight = jnp.concatenate(outs, axis=1).astype(f32)
    return (grad_input, grad_query, grad_key, grad_value, grad_weight)


def solution(mesh):
    in_specs = (
        P("seq", None),
        P("seq", "head"),
        P("seq", "head"),
        P("seq", "head"),
        P("seq", "head"),
        P("seq", "head"),
    )
    out_specs = (
        P("seq", "head"),
        P("seq", "head"),
        P("seq", "head"),
        P("seq", "head"),
        P("seq", "head"),
    )

    return jax.shard_map(local, mesh=mesh, in_specs=in_specs, out_specs=out_specs, check_vma=False)
```

profile of v0, /device:TPU:0, one launch (start us, length us, event | category | flops | bytes accessed | tf_op | source)
XLA Modules:
  0.0 200.3 jit_solution(4920119169477709384)
XLA Ops:
  0.6 3.0 %collective-permute-start.4 = (bf16[512,1024]{1,0:T(8,128)(2,1)}, bf16[512,1024]{1,0:T(8,128)(2,1)}, u32[]{:S(2)}, u32[]{:S(2)}) collective-permute-start(bf16[512,1024]{1,0:T(8,128)(2,1)} %param.11), channel_id=1, source_target_pairs={{0,8},{4,12},{8,0},{12,4},{16,24},{20,28},{24,16},{28,20},{1,9},{5... | collective-permute-start | bytes 3145736 | tf_op jit(solution)/shard_map/ppermute | solution.py:13
  3.7 1.5 copy.49
  5.2 1.5 copy.50
  6.7 1.2 fusion.102
  8.5 1.5 collective-permute-start.6
  10.0 0.8 iota_compare_fusion
  12.1 4.7 %fusion = f32[8,512,128]{1,2,0:T(8,128)} fusion(bf16[512,8,128]{0,2,1:T(8,128)(2,1)S(1)} %bitcast.92, f32[512]{0:T(512)S(1)} %multiply_rsqrt_fusion, pred[512,512]{1,0:T(8,128)(4,1)} %iota_compare_fusion, bf16[512,8,128]{0,2,1:T(8,128)(2,1)S(1)} %bitcast.89, bf16[512,1024]{1,0:T(8,128)(2,1)} %param.8), kind=kOutput, calls=%fused_computation.5 | convolution fusion | flops 1080033280 | bytes 5507072 | tf_op jit(solution)/shard_map/hts,thd->shd/dot_general | solution.py:102
  16.8 11.2 %collective-permute-done.4 = bf16[512,1024]{1,0:T(8,128)(2,1)} collective-permute-done((bf16[512,1024]{1,0:T(8,128)(2,1)}, bf16[512,1024]{1,0:T(8,128)(2,1)}, u32[]{:S(2)}, u32[]{:S(2)}) %collective-permute-start.4) | collective-permute-done | bytes 1048608 | tf_op jit(solution)/shard_map/ppermute | solution.py:13
  28.0 4.8 %collective-permute-done.1 = bf16[8,128,128]{1,2,0:T(8,128)(2,1)} collective-permute-done((bf16[8,128,128]{1,2,0:T(8,128)(2,1)}, bf16[8,128,128]{1,2,0:T(8,128)(2,1)}, u32[]{:S(2)}, u32[]{:S(2)}) %collective-permute-start.1) | collective-permute-done | bytes 262176 | tf_op jit(solution)/shard_map/ppermute | solution.py:13
  32.8 1.9 fusion.72
  34.7 1.8 collective-permute-start.2
  36.5 4.2 %constant_dynamic-slice_fusion.7 = (bf16[512,512]{1,0:T(8,128)(2,1)}, bf16[512,512]{1,0:T(8,128)(2,1)}, bf16[512,512]{1,0:T(8,128)(2,1)}, bf16[512,512]{1,0:T(8,...) fusion(bf16[512,4096]{1,0:T(8,128)(2,1)} %param.6, ...), kind=kLoop, calls=%fused_computation.127 | loop fusion | bytes 8388640 | tf_op jit(solution)/shard_map/dynamic_slice | solution.py:138
  40.7 1.4 constant_dynamic-update-slice_fusion.9
  42.2 1.1 slice.64
  43.2 1.6 collective-permute-start.8
  44.8 1.1 slice.65
  46.5 2.1 %fusion.22 = bf16[512,8,128]{0,2,1:T(8,128)(2,1)S(1)} fusion(f32[8,512,128]{1,2,0:T(8,128)S(1)} %copy-done.7, bf16[8,128,128]{1,2,0:T(8,128)(2,1)S(1)} %collective-permute-done, bf16[8,128,128]{1,2,0:T(8,128)(2,1)} %collective-permute-done.1, bf16[8,128,128]{1,2,0:T(8,128)(2,1)} %collective-permute-done.2, pred[]{:T(512)S(6)} %ne.26, pred[]{:T(512)S(6)} %ne.24, ...), kind=kOutput, calls=%fused_computation.30 | convolution fusion | flops 807403520 | bytes 4980739 | tf_op jit(solution)/shard_map/shi,hij->shj/dot_general | solution.py:103
  48.6 1.7 constant_dynamic-update-slice_fusion.8
  50.3 1.3 constant_dynamic-update-slice_fusion.7
  51.6 6.0 %collective-permute-done.8 = bf16[256,1024]{1,0:T(8,128)(2,1)S(1)} collective-permute-done((bf16[256,1024]{1,0:T(8,128)(2,1)S(1)}, bf16[256,1024]{1,0:T(8,128)(2,1)S(1)}, u32[]{:S(2)}, u32[]{:S(2)}) %collective-permute-start.8) | collective-permute-done | bytes 524320 | tf_op jit(solution)/shard_map/ppermute | solution.py:13
  57.6 2.4 %collective-permute-done.9 = bf16[256,1024]{1,0:T(8,128)(2,1)S(1)} collective-permute-done((bf16[256,1024]{1,0:T(8,128)(2,1)S(1)}, bf16[256,1024]{1,0:T(8,128)(2,1)S(1)}, u32[]{:S(2)}, u32[]{:S(2)}) %collective-permute-start.9) | collective-permute-done | bytes 524320 | tf_op jit(solution)/shard_map/ppermute | solution.py:13
  60.0 1.3 constant_dynamic-update-slice_fusion.6
  61.3 1.3 constant_dynamic-update-slice_fusion.5
  62.6 1.3 constant_dynamic-update-slice_fusion.4
  64.1 2.0 convolution_convert_fusion.6
  66.1 1.6 convolution_convert_fusion.5
  67.8 1.5 convolution_convert_fusion.4
  69.3 1.5 convolution_convert_fusion.3
  70.8 4.3 %multiply_convert_fusion = bf16[2048,1024]{0,1:T(8,128)(2,1)} fusion(bf16[512,1024]{0,1:T(8,128)(2,1)S(1)} %bitcast.99, bf16[512,512]{1,0:T(8,128)(2,1)S(1)} %copy-done.12, bf16[512,512]{1,0:T(8,128)(2,1)S(1)} %copy-done.13, bf16[512,512]{1,0:T(8,128)(2,1)S(1)} %copy-done.10, bf16[512,512]{1,0:T(8,128)(2,1)S(1)} %copy-done.11), kind=kOutput, calls=%fused_computation.1 | convolution fusion | flops 2160066560 | bytes 7340032 | tf_op jit(solution)/shard_map/dot_general | solution.py:140
  75.6 1.5 fusion.103
  77.1 2.8 %select_convert_fusion = bf16[8,512,512]{2,1,0:T(8,128)(2,1)S(1)} fusion(f32[512]{0:T(512)S(1)} %multiply_rsqrt_fusion, pred[512,512]{1,0:T(8,128)(4,1)} %iota_compare_fusion, bf16[512,8,128]{0,2,1:T(8,128)(2,1)S(1)} %bitcast.93, bf16[512,1024]{1,0:T(8,128)(2,1)S(1)} %copy-done), kind=kOutput, calls=%fused_computation.3 | convolution fusion | flops 543162368 | bytes 6555648 | tf_op jit(solution)/shard_map/thd,shd->hts/dot_general | solution.py:95
  79.9 3.2 %collective-permute-done.18 = bf16[8,128,128]{1,2,0:T(8,128)(2,1)} collective-permute-done((bf16[8,128,128]{1,2,0:T(8,128)(2,1)}, bf16[8,128,128]{1,2,0:T(8,128)(2,1)}, u32[]{:S(2)}, u32[]{:S(2)}) %collective-permute-start.18) | collective-permute-done | bytes 262176 | tf_op jit(solution)/shard_map/ppermute | solution.py:13
  83.1 1.0 fusion.80
  84.7 2.8 %fusion.49 = f32[8,512,128]{1,2,0:T(8,128)} fusion(bf16[8,512,512]{2,1,0:T(8,128)(2,1)S(1)} %select_convert_fusion, bf16[512,1024]{1,0:T(8,128)(2,1)S(1)} %copy-done.4), kind=kOutput, calls=%fused_computation.63 | convolution fusion | flops 536870912 | bytes 7340032 | tf_op jit(solution)/shard_map/hts,shd->thd/dot_general | solution.py:98
  87.6 5.2 %collective-permute-done.19 = bf16[8,128,128]{1,2,0:T(8,128)(2,1)S(1)} collective-permute-done((bf16[8,128,128]{1,2,0:T(8,128)(2,1)S(1)}, bf16[8,128,128]{1,2,0:T(8,128)(2,1)S(1)}, u32[]{:S(2)}, u32[]{:S(2)}) %collective-permute-start.19) | collective-permute-done | bytes 262176 | tf_op jit(solution)/shard_map/ppermute | solution.py:13
  92.8 1.8 fusion.76
  95.1 2.1 %fusion.104 = f32[8,512,128]{1,2,0:T(8,128)} fusion(bf16[512,8,128]{0,2,1:T(8,128)(2,1)S(1)} %bitcast.90, bf16[8,512,512]{2,1,0:T(8,128)(2,1)S(1)} %select_convert_fusion), kind=kOutput, calls=%fused_computation.146 | convolution fusion | flops 536870912 | bytes 7340032 | tf_op jit(solution)/shard_map/hts,thd->shd/dot_general | solution.py:100
  97.2 2.3 %copy.37 = bf16[512,1024]{1,0:T(8,128)(2,1)} copy(bf16[512,1024]{0,1:T(8,128)(2,1)} %bitcast.100) | data formatting | bytes 2097152
  99.5 3.2 %collective-permute-done.20 = bf16[8,128,128]{1,2,0:T(8,128)(2,1)} collective-permute-done((bf16[8,128,128]{1,2,0:T(8,128)(2,1)}, bf16[8,128,128]{1,2,0:T(8,128)(2,1)}, u32[]{:S(2)}, u32[]{:S(2)}) %collective-permute-start.20) | collective-permute-done | bytes 262176 | tf_op jit(solution)/shard_map/ppermute | solution.py:13
  102.7 3.0 %fusion.21 = bf16[512,8,128]{0,2,1:T(8,128)(2,1)S(1)} fusion(f32[8,512,128]{1,2,0:T(8,128)} %fusion.49, bf16[512,8,128]{0,2,1:T(8,128)(2,1)S(1)} %bitcast.94, f32[512]{0:T(512)S(1)} %multiply_rsqrt_fusion, bf16[8,128,128]{1,2,0:T(8,128)(2,1)} %collective-permute-done.18, bf16[8,128,128]{1,2,0:T(8,128)(2,1)} %copy-done.9, ...), kind=kOutput, calls=%fused_computation.28 | convolution fusion | flops 807927808 | bytes 4982787 | tf_op jit(solution)/shard_map/thj,hij->thi/dot_general | solution.py:99
  105.7 1.3 copy.35
  107.0 2.9 %fusion.20 = bf16[512,8,128]{0,2,1:T(8,128)(2,1)S(1)} fusion(f32[8,512,128]{1,2,0:T(8,128)} %fusion.104, bf16[8,128,128]{1,2,0:T(8,128)(2,1)S(1)} %collective-permute-done, bf16[8,128,128]{1,2,0:T(8,128)(2,1)} %collective-permute-done.1, bf16[8,128,128]{1,2,0:T(8,128)(2,1)} %collective-permute-done.2, pred[]{:T(512)S(6)} %ne.26, pred[]{:T(512)S(6)} %ne.24, ...), kind=kOutput, calls=%fused_computation.26 | convolution fusion | flops 807403520 | bytes 4980739 | tf_op jit(solution)/shard_map/shj,hij->shi/dot_general | solution.py:101
  109.9 1.3 copy.36
  111.2 1.6 collective-permute-start.16
  113.2 1.6 collective-permute-start.13
  115.2 5.2 %add_convert_fusion = bf16[2048,1024]{0,1:T(8,128)(2,1)S(1)} fusion(bf16[2048,1024]{0,1:T(8,128)(2,1)} %collective-permute-done.21, bf16[512,1024]{0,1:T(8,128)(2,1)S(1)} %bitcast.101, bf16[512,512]{1,0:T(8,128)(2,1)} %get-tuple-element.31, bf16[512,512]{1,0:T(8,128)(2,1)} %get-tuple-element.32, bf16[512,512]{1,0:T(8,128)(2,1)} %get-tuple-element.33, ...), kind=kOutput, calls=%fused_computation | convolution fusion | flops 2168455168 | bytes 11534336 | tf_op jit(solution)/shard_map/dot_general | solution.py:140
  120.4 1.4 fusion.101
  122.4 3.8 %collective-permute-done.16 = bf16[512,512]{0,1:T(8,128)(2,1)S(1)} collective-permute-done((bf16[512,512]{0,1:T(8,128)(2,1)}, bf16[512,512]{0,1:T(8,128)(2,1)S(1)}, u32[]{:S(2)}, u32[]{:S(2)}) %collective-permute-start.16) | collective-permute-done | bytes 524320 | tf_op jit(solution)/shard_map/ppermute | solution.py:13
  126.2 1.9 fusion.28
  128.1 2.7 %collective-permute-start.17 = (bf16[512,512]{0,1:T(8,128)(2,1)S(1)}, bf16[512,512]{0,1:T(8,128)(2,1)S(1)}, u32[]{:S(2)}, u32[]{:S(2)}) collective-permute-start(bf16[512,512]{0,1:T(8,128)(2,1)S(1)} %fusion.28), channel_id=1, source_target_pairs={{0,2},{1,3},{2,0},{3,1},{4,6},{5,7},{6,4},{7,5},{8,10},{9,11},{10,... | collective-permute-start | bytes 1572872 | tf_op jit(solution)/shard_map/ppermute | solution.py:13
  130.8 29.1 %collective-permute-done.13 = bf16[512,512]{0,1:T(8,128)(2,1)S(1)} collective-permute-done((bf16[512,512]{0,1:T(8,128)(2,1)}, bf16[512,512]{0,1:T(8,128)(2,1)S(1)}, u32[]{:S(2)}, u32[]{:S(2)}) %collective-permute-start.13) | collective-permute-done | bytes 524320 | tf_op jit(solution)/shard_map/ppermute | solution.py:13
  160.4 1.9 fusion.35
  162.3 1.8 collective-permute-start.14
  164.2 0.9 add_convert_fusion.2
  165.1 5.4 %collective-permute-done.26 = bf16[512,512]{0,1:T(8,128)(2,1)S(1)} collective-permute-done((bf16[512,512]{0,1:T(8,128)(2,1)S(1)}, bf16[512,512]{0,1:T(8,128)(2,1)S(1)}, u32[]{:S(2)}, u32[]{:S(2)}) %collective-permute-start.26) | collective-permute-done | bytes 524320 | tf_op jit(solution)/shard_map/ppermute | solution.py:13
  170.6 0.9 add_convert_fusion.1
  172.1 1.4 collective-permute-start.24
  173.5 2.0 %collective-permute-start.27 = (bf16[512,512]{0,1:T(8,128)(2,1)}, bf16[512,512]{0,1:T(8,128)(2,1)}, u32[]{:S(2)}, u32[]{:S(2)}) collective-permute-start(bf16[512,512]{0,1:T(8,128)(2,1)} %add_convert_fusion.1), channel_id=1, source_target_pairs={{0,8},{4,12},{8,0},{12,4},{16,24},{20,28},{24,16},{28,20},{1,9},{5... | collective-permute-start | bytes 1572872 | tf_op jit(solution)/shard_map/ppermute | solution.py:13
  175.6 2.0 fusion.32
  177.5 15.4 %collective-permute-done.14 = bf16[512,512]{0,1:T(8,128)(2,1)S(1)} collective-permute-done((bf16[512,512]{0,1:T(8,128)(2,1)S(1)}, bf16[512,512]{0,1:T(8,128)(2,1)S(1)}, u32[]{:S(2)}, u32[]{:S(2)}) %collective-permute-start.14) | collective-permute-done | bytes 524320 | tf_op jit(solution)/shard_map/ppermute | solution.py:13
  192.9 2.0 fusion.39
  195.0 1.3 copy.34
  196.3 2.0 convert_add_fusion.1
  198.4 1.8 copy.38
  (73 shorter events, 7.1 us)
Async XLA Ops:
  0.6 75.0 %copy-start = (bf16[512,1024]{1,0:T(8,128)(2,1)S(1)}, bf16[512,1024]{1,0:T(8,128)(2,1)}, u32[]{:S(2)}) copy-start(bf16[512,1024]{1,0:T(8,128)(2,1)} %param.9) | copy-start | bytes 3145732
  0.6 27.4 %collective-permute-start.4 = (bf16[512,1024]{1,0:T(8,128)(2,1)}, bf16[512,1024]{1,0:T(8,128)(2,1)}, u32[]{:S(2)}, u32[]{:S(2)}) collective-permute-start(bf16[512,1024]{1,0:T(8,128)(2,1)} %param.11), channel_id=1, source_target_pairs={{0,8},{4,12},{8,0},{12,4},{16,24},{20,28},{24,16},{28,20},{1,9},{5... | collective-permute-start | bytes 3145736 | tf_op jit(solution)/shard_map/ppermute | solution.py:13
  7.9 2.9 %copy-start.1 = (f32[8,128,128]{1,2,0:T(8,128)}, f32[8,128,128]{1,2,0:T(8,128)S(1)}, u32[]{:S(2)}) copy-start(f32[8,128,128]{1,2,0:T(8,128)S(1)} %get-tuple-element.37) | copy-start | bytes 1572868
  7.9 2.9 %collective-permute-start = (bf16[8,128,128]{1,2,0:T(8,128)(2,1)S(1)}, bf16[8,128,128]{1,2,0:T(8,128)(2,1)S(1)}, u32[]{:S(2)}, u32[]{:S(2)}) collective-permute-start(bf16[8,128,128]{1,2,0:T(8,128)(2,1)S(1)} %get-tuple-element.36), channel_id=1, source_target_pairs={{0,4},{4,0},{8,12},{12,8},{16,20},{20,16},{24,28},{28,24},{1,5},{5... | collective-permute-start | bytes 786440 | tf_op jit(solution)/shard_map/ppermute | solution.py:13
  8.0 40.6 %collective-permute-start.3 = (bf16[512,1024]{1,0:T(8,128)(2,1)}, bf16[512,1024]{1,0:T(8,128)(2,1)}, u32[]{:S(2)}, u32[]{:S(2)}) collective-permute-start(bf16[512,1024]{1,0:T(8,128)(2,1)} %param.11), channel_id=1, source_target_pairs={{0,4},{4,0},{8,12},{12,8},{16,20},{20,16},{24,28},{28,24},{1,5},{5... | collective-permute-start | bytes 3145736 | tf_op jit(solution)/shard_map/ppermute | solution.py:13
  8.5 28.0 %collective-permute-start.6 = (bf16[512,1024]{1,0:T(8,128)(2,1)}, bf16[512,1024]{1,0:T(8,128)(2,1)}, u32[]{:S(2)}, u32[]{:S(2)}) collective-permute-start(bf16[512,1024]{1,0:T(8,128)(2,1)} %param.11), channel_id=1, source_target_pairs={{0,16},{4,20},{8,24},{12,28},{16,0},{20,4},{24,8},{28,12},{1,17},{... | collective-permute-start | bytes 3145736 | tf_op jit(solution)/shard_map/ppermute | solution.py:13
  11.6 21.2 %collective-permute-start.1 = (bf16[8,128,128]{1,2,0:T(8,128)(2,1)}, bf16[8,128,128]{1,2,0:T(8,128)(2,1)}, u32[]{:S(2)}, u32[]{:S(2)}) collective-permute-start(bf16[8,128,128]{1,2,0:T(8,128)(2,1)} %fusion.79), channel_id=1, source_target_pairs={{0,8},{4,12},{8,0},{12,4},{16,24},{20,28},{24,16},{28,20},{1,9},{5... | collective-permute-start | bytes 786440 | tf_op jit(solution)/shard_map/ppermute | solution.py:13
  28.0 32.0 %collective-permute-start.5 = (bf16[512,1024]{1,0:T(8,128)(2,1)}, bf16[512,1024]{1,0:T(8,128)(2,1)}, u32[]{:S(2)}, u32[]{:S(2)}) collective-permute-start(bf16[512,1024]{1,0:T(8,128)(2,1)} %collective-permute-done.4), channel_id=1, source_target_pairs={{0,4},{4,0},{8,12},{12,8},{16,20},{20,16},{24,28},{28,24},{1,5},{5... | collective-permute-start | bytes 3145736 | tf_op jit(solution)/shard_map/ppermute | solution.py:13
  34.7 11.2 %collective-permute-start.2 = (bf16[8,128,128]{1,2,0:T(8,128)(2,1)}, bf16[8,128,128]{1,2,0:T(8,128)(2,1)}, u32[]{:S(2)}, u32[]{:S(2)}) collective-permute-start(bf16[8,128,128]{1,2,0:T(8,128)(2,1)} %fusion.72), channel_id=1, source_target_pairs={{0,16},{4,20},{8,24},{12,28},{16,0},{20,4},{24,8},{28,12},{1,17},{... | collective-permute-start | bytes 786440 | tf_op jit(solution)/shard_map/ppermute | solution.py:13
  36.5 26.1 %collective-permute-start.7 = (bf16[512,1024]{1,0:T(8,128)(2,1)}, bf16[512,1024]{1,0:T(8,128)(2,1)}, u32[]{:S(2)}, u32[]{:S(2)}) collective-permute-start(bf16[512,1024]{1,0:T(8,128)(2,1)} %collective-permute-done.6), channel_id=1, source_target_pairs={{0,4},{4,0},{8,12},{12,8},{16,20},{20,16},{24,28},{28,24},{1,5},{5... | collective-permute-start | bytes 3145736 | tf_op jit(solution)/shard_map/ppermute | solution.py:13
  40.7 5.8 %copy-start.3 = (bf16[512,1024]{1,0:T(8,128)(2,1)S(1)}, bf16[512,1024]{1,0:T(8,128)(2,1)}, u32[]{:S(2)}) copy-start(bf16[512,1024]{1,0:T(8,128)(2,1)} %param.8) | copy-start | bytes 3145732
  40.7 5.8 %copy-start.7 = (f32[8,512,128]{1,2,0:T(8,128)S(1)}, f32[8,512,128]{1,2,0:T(8,128)}, u32[]{:S(2)}) copy-start(f32[8,512,128]{1,2,0:T(8,128)} %fusion) | copy-start | bytes 6291460
  43.2 14.4 %collective-permute-start.8 = (bf16[256,1024]{1,0:T(8,128)(2,1)S(1)}, bf16[256,1024]{1,0:T(8,128)(2,1)S(1)}, u32[]{:S(2)}, u32[]{:S(2)}) collective-permute-start(bf16[256,1024]{1,0:T(8,128)(2,1)S(1)} %slice.64), channel_id=1, source_target_pairs={{0,8},{4,12},{8,0},{12,4},{16,24},{20,28},{24,16},{28,20},{1,9},{5... | collective-permute-start | bytes 1572872 | tf_op jit(solution)/shard_map/ppermute | solution.py:13
  45.9 14.1 %collective-permute-start.9 = (bf16[256,1024]{1,0:T(8,128)(2,1)S(1)}, bf16[256,1024]{1,0:T(8,128)(2,1)S(1)}, u32[]{:S(2)}, u32[]{:S(2)}) collective-permute-start(bf16[256,1024]{1,0:T(8,128)(2,1)S(1)} %slice.65), channel_id=1, source_target_pairs={{0,16},{4,20},{8,24},{12,28},{16,0},{20,4},{24,8},{28,12},{1,17},{... | collective-permute-start | bytes 1572872 | tf_op jit(solution)/shard_map/ppermute | solution.py:13
  48.6 22.2 %copy-start.5 = (bf16[512,8,128]{0,2,1:T(8,128)(2,1)}, bf16[512,8,128]{0,2,1:T(8,128)(2,1)S(1)}, u32[]{:S(2)}) copy-start(bf16[512,8,128]{0,2,1:T(8,128)(2,1)S(1)} %fusion.22) | copy-start | bytes 3145732
  57.6 6.4 %collective-permute-start.10 = (bf16[256,1024]{1,0:T(8,128)(2,1)S(1)}, bf16[256,1024]{1,0:T(8,128)(2,1)S(1)}, u32[]{:S(2)}, u32[]{:S(2)}) collective-permute-start(bf16[256,1024]{1,0:T(8,128)(2,1)S(1)} %collective-permute-done.8), channel_id=1, source_target_pairs={{0,4},{4,0},{8,12},{12,8},{16,20},{20,16},{24,28},{28,24},{1,5},{5... | collective-permute-start | bytes 1572872 | tf_op jit(solution)/shard_map/ppermute | solution.py:13
  60.0 4.1 %collective-permute-start.11 = (bf16[256,1024]{1,0:T(8,128)(2,1)S(1)}, bf16[256,1024]{1,0:T(8,128)(2,1)S(1)}, u32[]{:S(2)}, u32[]{:S(2)}) collective-permute-start(bf16[256,1024]{1,0:T(8,128)(2,1)S(1)} %collective-permute-done.9), channel_id=1, source_target_pairs={{0,4},{4,0},{8,12},{12,8},{16,20},{20,16},{24,28},{28,24},{1,5},{5... | collective-permute-start | bytes 1572872 | tf_op jit(solution)/shard_map/ppermute | solution.py:13
  64.1 5.2 %copy-start.14 = (bf16[4096,1024]{1,0:T(8,128)(2,1)}, bf16[4096,1024]{1,0:T(8,128)(2,1)S(1)}, u32[]{:S(2)}) copy-start(bf16[4096,1024]{1,0:T(8,128)(2,1)S(1)} %constant_dynamic-update-slice_fusion) | copy-start | bytes 25165828
  67.8 3.1 %copy-start.10 = (bf16[512,512]{1,0:T(8,128)(2,1)S(1)}, bf16[512,512]{1,0:T(8,128)(2,1)}, u32[]{:S(2)}) copy-start(bf16[512,512]{1,0:T(8,128)(2,1)} %get-tuple-element.29) | copy-start | bytes 1572868
  67.8 3.1 %copy-start.11 = (bf16[512,512]{1,0:T(8,128)(2,1)S(1)}, bf16[512,512]{1,0:T(8,128)(2,1)}, u32[]{:S(2)}) copy-start(bf16[512,512]{1,0:T(8,128)(2,1)} %get-tuple-element.30) | copy-start | bytes 1572868
  67.8 3.1 %copy-start.12 = (bf16[512,512]{1,0:T(8,128)(2,1)S(1)}, bf16[512,512]{1,0:T(8,128)(2,1)}, u32[]{:S(2)}) copy-start(bf16[512,512]{1,0:T(8,128)(2,1)} %get-tuple-element.34) | copy-start | bytes 1572868
  67.8 3.1 %copy-start.13 = (bf16[512,512]{1,0:T(8,128)(2,1)S(1)}, bf16[512,512]{1,0:T(8,128)(2,1)}, u32[]{:S(2)}) copy-start(bf16[512,512]{1,0:T(8,128)(2,1)} %get-tuple-element.35) | copy-start | bytes 1572868
  75.1 40.1 %collective-permute-start.21 = (bf16[2048,1024]{0,1:T(8,128)(2,1)}, bf16[2048,1024]{0,1:T(8,128)(2,1)}, u32[]{:S(2)}, u32[]{:S(2)}) collective-permute-start(bf16[2048,1024]{0,1:T(8,128)(2,1)} %multiply_convert_fusion), channel_id=1, source_target_pairs={{0,4},{4,0},{8,12},{12,8},{16,20},{20,16},{24,28},{28,24},{1,5},{5... | collective-permute-start | bytes 12582920 | tf_op jit(solution)/shard_map/ppermute | solution.py:13
  77.1 6.0 %collective-permute-start.18 = (bf16[8,128,128]{1,2,0:T(8,128)(2,1)}, bf16[8,128,128]{1,2,0:T(8,128)(2,1)}, u32[]{:S(2)}, u32[]{:S(2)}) collective-permute-start(bf16[8,128,128]{1,2,0:T(8,128)(2,1)} %get-tuple-element.38), channel_id=1, source_target_pairs={{0,4},{4,0},{8,12},{12,8},{16,20},{20,16},{24,28},{28,24},{1,5},{5... | collective-permute-start | bytes 786440 | tf_op jit(solution)/shard_map/ppermute | solution.py:13
  77.1 6.0 %copy-start.8 = (f32[8,128,128]{1,2,0:T(8,128)S(1)}, f32[8,128,128]{1,2,0:T(8,128)}, u32[]{:S(2)}) copy-start(f32[8,128,128]{1,2,0:T(8,128)} %get-tuple-element.39) | copy-start | bytes 1572868
  77.1 7.7 %copy-start.4 = (bf16[512,1024]{1,0:T(8,128)(2,1)S(1)}, bf16[512,1024]{1,0:T(8,128)(2,1)}, u32[]{:S(2)}) copy-start(bf16[512,1024]{1,0:T(8,128)(2,1)} %param.8) | copy-start | bytes 3145732
  84.1 8.7 %collective-permute-start.19 = (bf16[8,128,128]{1,2,0:T(8,128)(2,1)S(1)}, bf16[8,128,128]{1,2,0:T(8,128)(2,1)S(1)}, u32[]{:S(2)}, u32[]{:S(2)}) collective-permute-start(bf16[8,128,128]{1,2,0:T(8,128)(2,1)S(1)} %fusion.80), channel_id=1, source_target_pairs={{0,8},{4,12},{8,0},{12,4},{16,24},{20,28},{24,16},{28,20},{1,9},{5... | collective-permute-start | bytes 786440 | tf_op jit(solution)/shard_map/ppermute | solution.py:13
  92.8 1.8 copy-start.9
  94.6 8.0 %collective-permute-start.20 = (bf16[8,128,128]{1,2,0:T(8,128)(2,1)}, bf16[8,128,128]{1,2,0:T(8,128)(2,1)}, u32[]{:S(2)}, u32[]{:S(2)}) collective-permute-start(bf16[8,128,128]{1,2,0:T(8,128)(2,1)} %fusion.76), channel_id=1, source_target_pairs={{0,16},{4,20},{8,24},{12,28},{16,0},{20,4},{24,8},{28,12},{1,17},{... | collective-permute-start | bytes 786440 | tf_op jit(solution)/shard_map/ppermute | solution.py:13
  105.6 9.6 %copy-start.6 = (bf16[512,8,128]{0,2,1:T(8,128)(2,1)S(1)}, bf16[512,8,128]{0,2,1:T(8,128)(2,1)}, u32[]{:S(2)}) copy-start(bf16[512,8,128]{0,2,1:T(8,128)(2,1)} %copy-done.5) | copy-start | bytes 3145732
  111.2 15.0 %collective-permute-start.16 = (bf16[512,512]{0,1:T(8,128)(2,1)}, bf16[512,512]{0,1:T(8,128)(2,1)S(1)}, u32[]{:S(2)}, u32[]{:S(2)}) collective-permute-start(bf16[512,512]{0,1:T(8,128)(2,1)} %convolution_convert_fusion.3), channel_id=1, source_target_pairs={{0,1},{1,0},{2,3},{3,2},{4,5},{5,4},{6,7},{7,6},{8,9},{9,8},{10,11... | collective-permute-start | bytes 1572872 | tf_op jit(solution)/shard_map/ppermute | solution.py:13
  112.7 58.8 %collective-permute-start.15 = (bf16[512,512]{0,1:T(8,128)(2,1)}, bf16[512,512]{0,1:T(8,128)(2,1)S(1)}, u32[]{:S(2)}, u32[]{:S(2)}) collective-permute-start(bf16[512,512]{0,1:T(8,128)(2,1)} %convolution_convert_fusion.5), channel_id=1, source_target_pairs={{0,1},{1,0},{2,3},{3,2},{4,5},{5,4},{6,7},{7,6},{8,9},{9,8},{10,11... | collective-permute-start | bytes 1572872 | tf_op jit(solution)/shard_map/ppermute | solution.py:13
  113.2 46.7 %collective-permute-start.13 = (bf16[512,512]{0,1:T(8,128)(2,1)}, bf16[512,512]{0,1:T(8,128)(2,1)S(1)}, u32[]{:S(2)}, u32[]{:S(2)}) collective-permute-start(bf16[512,512]{0,1:T(8,128)(2,1)} %convolution_convert_fusion.4), channel_id=1, source_target_pairs={{0,1},{1,0},{2,3},{3,2},{4,5},{5,4},{6,7},{7,6},{8,9},{9,8},{10,11... | collective-permute-start | bytes 1572872 | tf_op jit(solution)/shard_map/ppermute | solution.py:13
  114.8 57.3 %collective-permute-start.12 = (bf16[512,512]{0,1:T(8,128)(2,1)}, bf16[512,512]{0,1:T(8,128)(2,1)S(1)}, u32[]{:S(2)}, u32[]{:S(2)}) collective-permute-start(bf16[512,512]{0,1:T(8,128)(2,1)} %convolution_convert_fusion.6), channel_id=1, source_target_pairs={{0,1},{1,0},{2,3},{3,2},{4,5},{5,4},{6,7},{7,6},{8,9},{9,8},{10,11... | collective-permute-start | bytes 1572872 | tf_op jit(solution)/shard_map/ppermute | solution.py:13
  120.4 7.7 %copy-start.2 = (bf16[2048,1024]{0,1:T(8,128)(2,1)}, bf16[2048,1024]{0,1:T(8,128)(2,1)S(1)}, u32[]{:S(2)}) copy-start(bf16[2048,1024]{0,1:T(8,128)(2,1)S(1)} %add_convert_fusion) | copy-start | bytes 12582916
  121.8 40.5 %collective-permute-start.23 = (bf16[512,512]{0,1:T(8,128)(2,1)S(1)}, bf16[512,512]{0,1:T(8,128)(2,1)S(1)}, u32[]{:S(2)}, u32[]{:S(2)}) collective-permute-start(bf16[512,512]{0,1:T(8,128)(2,1)S(1)} %get-tuple-element.26), channel_id=1, source_target_pairs={{0,8},{4,12},{8,0},{12,4},{16,24},{20,28},{24,16},{28,20},{1,9},{5... | collective-permute-start | bytes 1572872 | tf_op jit(solution)/shard_map/ppermute | solution.py:13
  128.1 45.4 %collective-permute-start.17 = (bf16[512,512]{0,1:T(8,128)(2,1)S(1)}, bf16[512,512]{0,1:T(8,128)(2,1)S(1)}, u32[]{:S(2)}, u32[]{:S(2)}) collective-permute-start(bf16[512,512]{0,1:T(8,128)(2,1)S(1)} %fusion.28), channel_id=1, source_target_pairs={{0,2},{1,3},{2,0},{3,1},{4,6},{5,7},{6,4},{7,5},{8,10},{9,11},{10,... | collective-permute-start | bytes 1572872 | tf_op jit(solution)/shard_map/ppermute | solution.py:13
  159.9 10.7 %collective-permute-start.26 = (bf16[512,512]{0,1:T(8,128)(2,1)S(1)}, bf16[512,512]{0,1:T(8,128)(2,1)S(1)}, u32[]{:S(2)}, u32[]{:S(2)}) collective-permute-start(bf16[512,512]{0,1:T(8,128)(2,1)S(1)} %get-tuple-element.23), channel_id=1, source_target_pairs={{0,16},{4,20},{8,24},{12,28},{16,0},{20,4},{24,8},{28,12},{1,17},{... | collective-permute-start | bytes 1572872 | tf_op jit(solution)/shard_map/ppermute | solution.py:13
  162.3 30.6 %collective-permute-start.14 = (bf16[512,512]{0,1:T(8,128)(2,1)S(1)}, bf16[512,512]{0,1:T(8,128)(2,1)S(1)}, u32[]{:S(2)}, u32[]{:S(2)}) collective-permute-start(bf16[512,512]{0,1:T(8,128)(2,1)S(1)} %fusion.35), channel_id=1, source_target_pairs={{0,2},{1,3},{2,0},{3,1},{4,6},{5,7},{6,4},{7,5},{8,10},{9,11},{10,... | collective-permute-start | bytes 1572872 | tf_op jit(solution)/shard_map/ppermute | solution.py:13
  170.6 25.7 %collective-permute-start.22 = (bf16[512,512]{0,1:T(8,128)(2,1)}, bf16[512,512]{0,1:T(8,128)(2,1)S(1)}, u32[]{:S(2)}, u32[]{:S(2)}) collective-permute-start(bf16[512,512]{0,1:T(8,128)(2,1)} %get-tuple-element.22), channel_id=1, source_target_pairs={{0,8},{4,12},{8,0},{12,4},{16,24},{20,28},{24,16},{28,20},{1,9},{5... | collective-permute-start | bytes 1572872 | tf_op jit(solution)/shard_map/ppermute | solution.py:13
  171.5 24.8 %collective-permute-start.25 = (bf16[512,512]{0,1:T(8,128)(2,1)}, bf16[512,512]{0,1:T(8,128)(2,1)S(1)}, u32[]{:S(2)}, u32[]{:S(2)}) collective-permute-start(bf16[512,512]{0,1:T(8,128)(2,1)} %get-tuple-element.25), channel_id=1, source_target_pairs={{0,16},{4,20},{8,24},{12,28},{16,0},{20,4},{24,8},{28,12},{1,17},{... | collective-permute-start | bytes 1572872 | tf_op jit(solution)/shard_map/ppermute | solution.py:13
  172.1 24.2 %collective-permute-start.24 = (bf16[512,512]{0,1:T(8,128)(2,1)}, bf16[512,512]{0,1:T(8,128)(2,1)}, u32[]{:S(2)}, u32[]{:S(2)}) collective-permute-start(bf16[512,512]{0,1:T(8,128)(2,1)} %add_convert_fusion.2), channel_id=1, source_target_pairs={{0,16},{4,20},{8,24},{12,28},{16,0},{20,4},{24,8},{28,12},{1,17},{... | collective-permute-start | bytes 1572872 | tf_op jit(solution)/shard_map/ppermute | solution.py:13
  173.5 22.8 %collective-permute-start.27 = (bf16[512,512]{0,1:T(8,128)(2,1)}, bf16[512,512]{0,1:T(8,128)(2,1)}, u32[]{:S(2)}, u32[]{:S(2)}) collective-permute-start(bf16[512,512]{0,1:T(8,128)(2,1)} %add_convert_fusion.1), channel_id=1, source_target_pairs={{0,8},{4,12},{8,0},{12,4},{16,24},{20,28},{24,16},{28,20},{1,9},{5... | collective-permute-start | bytes 1572872 | tf_op jit(solution)/shard_map/ppermute | solution.py:13
where the time goes:
time: 201 us; the launch traced here: 200 us
  waiting for transfers between devices  89.7 us (45%)
  matrix products  47 us (23%)
  local copies, waits for them, and re-layouts  27.3 us (14%)
  starting transfers between devices  24.8 us (12%)
  other arithmetic  10.4 us (5%)
    ppermute x28, waiting for transfers between devices, exchange(): lax.ppermute(x, axis, [(i, i ^ bit) for i in range(lax.axis_size(axis))])  89.7 us
    ppermute x28, starting transfers between devices, exchange(): lax.ppermute(x, axis, [(i, i ^ bit) for i in range(lax.axis_size(axis))])  24.8 us
    unnamed x44, local copies, waits for them, and re-layouts  16.5 us
    dot_general x8, matrix products, local(): lax.dot_general(grad_value, part, (((1,), (1,)), ((), ())), preferred_ele...  14.5 us
    dot_general x2, matrix products, local(): lax.dot_general(picked, late_value, (((0,), (0,)), ((), ())), preferred_e...  9.45 us
    convert_element_type x4, other arithmetic, carried_in(): got = exchange(total.astype(jnp.bfloat16), axis, bit).astype(state.dtype)  5.55 us
    dot_general x1, matrix products, local(): dv = jnp.einsum('hts,thd->shd', score_qk, o3, preferred_element_type=f32)  4.74 us
    dynamic_slice x1, local copies, waits for them, and re-layouts, local(): lax.dynamic_slice_in_dim(inputs, (here ^ m) * slab, slab, 1)  4.24 us
  transfers between devices with their start and end apart: 28, of which 11 were waited for; matrix products, arithmetic and copies ran while one was open for 35% of the time, Pallas kernels for 0%

commit v1 on v0

--- a/solution.py
+++ b/solution.py
@@ -19,15 +19,17 @@
     return [1 << k for k in range(count.bit_length() - 1)]
 
 
-def carried_in(state, axis, later):
+def carried_in(forward, backward, axis):
     here = lax.axis_index(axis)
-    carried, total = jnp.zeros_like(state), state
+    total = jnp.stack([forward, backward])
+    carried = jnp.zeros_like(total)
     for bit in bits_of(axis):
-        got = exchange(total.astype(jnp.bfloat16), axis, bit).astype(state.dtype)
+        got = exchange(total.astype(jnp.bfloat16), axis, bit).astype(total.dtype)
         upper = (here & bit) != 0
-        carried = carried + jnp.where(upper != later, got, 0.0)
+        wanted = jnp.stack([upper, ~upper])[:, None, None, None]
+        carried = carried + jnp.where(wanted, got, 0.0)
         total = total + got
-    return carried
+    return carried[0], carried[1]
 
 
 def halving(terms, axis, bits):
@@ -83,8 +85,7 @@
     state_qo = jnp.einsum(
         "thi,thj->hij", q3.astype(f32), o3wide * factor[:, None, None], precision=high
     )
-    suffix = carried_in(state_qo, "seq", True)
-    prefix = carried_in(state_kv, "seq", False)
+    prefix, suffix = carried_in(state_kv, state_qo, "seq")
     index = jnp.arange(rows, dtype=jnp.int32)
     lower = (index[:, None] >= index[None, :])[None]
     score_qk = (

time: 201 us -> 202 us (level)
    ppermute x28 -> x25, starting transfers between devices: 24.8 us -> 26 us  [exchange(): lax.ppermute(x, axis, [(i, i ^ bit) for i in range(lax.axis_size(axis))])]
    convert_element_type x4 -> x3, other arithmetic: 5.55 us -> 4.54 us  [carried_in(): got = exchange(total.astype(jnp.bfloat16), axis, bit).astype(total.dtype)]
    ppermute x28 -> x25, waiting for transfers between devices: 89.7 us -> 89 us  [exchange(): lax.ppermute(x, axis, [(i, i ^ bit) for i in range(lax.axis_size(axis))])]
    unnamed x44 -> x50, local copies, waits for them, and re-layouts: 16.5 us -> 16.8 us
  transfers between devices with their start and end apart: 28 -> 25, of which waited for: 11 -> 7; matrix products, arithmetic and copies ran while one was open for 35% -> 31% of each run, Pallas kernels for 0% -> 0%
where the time goes in v1:
time: 202 us; the launch traced here: 201 us
  waiting for transfers between devices  89 us (44%)
  matrix products  47 us (23%)
  local copies, waits for them, and re-layouts  27.9 us (14%)
  starting transfers between devices  26 us (13%)
  other arithmetic  10.4 us (5%)
    ppermute x25, waiting for transfers between devices, exchange(): lax.ppermute(x, axis, [(i, i ^ bit) for i in range(lax.axis_size(axis))])  89 us
    ppermute x25, starting transfers between devices, exchange(): lax.ppermute(x, axis, [(i, i ^ bit) for i in range(lax.axis_size(axis))])  26 us
    unnamed x50, local copies, waits for them, and re-layouts  16.8 us
    dot_general x8, matrix products, local(): lax.dot_general(grad_value, part, (((1,), (1,)), ((), ())), preferred_ele...  14.4 us
    dot_general x2, matrix products, local(): lax.dot_general(picked, late_value, (((0,), (0,)), ((), ())), preferred_e...  9.5 us
    dot_general x1, matrix products, local(): dv = jnp.einsum('hts,thd->shd', score_qk, o3, preferred_element_type=f32)  4.7 us
    convert_element_type x3, other arithmetic, carried_in(): got = exchange(total.astype(jnp.bfloat16), axis, bit).astype(total.dtype)  4.54 us
    dynamic_slice x1, local copies, waits for them, and re-layouts, local(): lax.dynamic_slice_in_dim(inputs, (here ^ m) * slab, slab, 1)  4.37 us
  transfers between devices with their start and end apart: 25, of which 7 were waited for; matrix products, arithmetic and copies ran while one was open for 31% of the time, Pallas kernels for 0%

profile of v1, /device:TPU:0, one launch (start us, length us, event | category | flops | bytes accessed | tf_op | source)
XLA Modules:
  0.0 201.3 jit_solution(8369122731051306884)
XLA Ops:
  0.7 1.6 copy.46
  2.3 1.5 copy.47
  3.8 1.8 convolution_bitcast_fusion
  5.5 1.4 fusion.40
  6.9 0.8 copy-done.1
  7.7 0.9 fusion.64
  9.1 3.0 %collective-permute-start.4 = (bf16[512,1024]{1,0:T(8,128)(2,1)}, bf16[512,1024]{1,0:T(8,128)(2,1)}, u32[]{:S(2)}, u32[]{:S(2)}) collective-permute-start(bf16[512,1024]{1,0:T(8,128)(2,1)} %param.11), channel_id=1, source_target_pairs={{0,8},{4,12},{8,0},{12,4},{16,24},{20,28},{24,16},{28,20},{1,9},{5... | collective-permute-start | bytes 3145736 | tf_op jit(solution)/shard_map/ppermute | solution.py:13
  12.1 1.5 collective-permute-start.6
  13.7 4.4 %constant_dynamic-slice_fusion.7 = (bf16[512,512]{1,0:T(8,128)(2,1)}, bf16[512,512]{1,0:T(8,128)(2,1)}, bf16[512,512]{1,0:T(8,128)(2,1)}, bf16[512,512]{1,0:T(8,...) fusion(bf16[512,4096]{1,0:T(8,128)(2,1)} %param.6, ...), kind=kLoop, calls=%fused_computation.117 | loop fusion | bytes 8388640 | tf_op jit(solution)/shard_map/dynamic_slice | solution.py:139
  18.1 2.0 fusion.73
  20.1 0.5 collective-permute-start.1
  20.7 4.7 %fusion = f32[8,512,128]{1,2,0:T(8,128)} fusion(bf16[512,8,128]{0,2,1:T(8,128)(2,1)S(1)} %bitcast.105, f32[512]{0:T(512)S(1)} %multiply_rsqrt_fusion, pred[512,512]{1,0:T(8,128)(4,1)S(1)} %iota_compare_fusion, bf16[512,8,128]{0,2,1:T(8,128)(2,1)S(1)} %bitcast.102, bf16[512,1024]{1,0:T(8,128)(2,1)} %param.8), kind=kOutput, calls=%fused_computation.5 | convolution fusion | flops 1080033280 | bytes 5507072 | tf_op jit(solution)/shard_map/hts,thd->shd/dot_general | solution.py:103
  25.4 21.6 %collective-permute-done.1 = bf16[2,8,128,128]{3,2,1,0:T(8,128)(2,1)} collective-permute-done((bf16[2,8,128,128]{3,2,1,0:T(8,128)(2,1)}, bf16[2,8,128,128]{3,2,1,0:T(8,128)(2,1)}, u32[]{:S(2)}, u32[]{:S(2)}) %collective-permute-start.1) | collective-permute-done | bytes 524320 | tf_op jit(solution)/shard_map/ppermute | solution.py:13
  47.0 1.7 fusion.45
  48.7 1.8 collective-permute-start.2
  50.5 1.1 slice.72
  51.6 1.6 collective-permute-start.8
  53.1 1.1 slice.73
  54.2 0.6 collective-permute-start.9
  54.9 1.4 constant_dynamic-update-slice_fusion.9
  56.8 1.3 constant_dynamic-update-slice_fusion.8
  58.1 1.3 constant_dynamic-update-slice_fusion.7
  59.4 5.0 %collective-permute-done.8 = bf16[256,1024]{1,0:T(8,128)(2,1)S(1)} collective-permute-done((bf16[256,1024]{1,0:T(8,128)(2,1)S(1)}, bf16[256,1024]{1,0:T(8,128)(2,1)S(1)}, u32[]{:S(2)}, u32[]{:S(2)}) %collective-permute-start.8) | collective-permute-done | bytes 524320 | tf_op jit(solution)/shard_map/ppermute | solution.py:13
  64.3 8.9 %collective-permute-done.9 = bf16[256,1024]{1,0:T(8,128)(2,1)S(1)} collective-permute-done((bf16[256,1024]{1,0:T(8,128)(2,1)S(1)}, bf16[256,1024]{1,0:T(8,128)(2,1)S(1)}, u32[]{:S(2)}, u32[]{:S(2)}) %collective-permute-start.9) | collective-permute-done | bytes 524320 | tf_op jit(solution)/shard_map/ppermute | solution.py:13
  73.2 1.5 fusion.44
  74.8 1.2 fusion.22
  76.1 1.6 constant_dynamic-update-slice_fusion.5
  78.0 2.0 convolution_convert_fusion.6
  80.0 1.7 convolution_convert_fusion.5
  81.6 1.5 convolution_convert_fusion.4
  83.1 1.5 convolution_convert_fusion.3
  84.7 4.3 %multiply_convert_fusion = bf16[2048,1024]{0,1:T(8,128)(2,1)} fusion(bf16[512,1024]{0,1:T(8,128)(2,1)S(1)} %bitcast.112, bf16[512,512]{1,0:T(8,128)(2,1)S(1)} %copy-done.15, bf16[512,512]{1,0:T(8,128)(2,1)S(1)} %copy-done.16, bf16[512,512]{1,0:T(8,128)(2,1)S(1)} %copy-done.13, bf16[512,512]{1,0:T(8,128)(2,1)S(1)} %copy-done.14), kind=kOutput, calls=%fused_computation.1 | convolution fusion | flops 2160066560 | bytes 7340032 | tf_op jit(solution)/shard_map/dot_general | solution.py:141
  89.5 1.7 select_convert_fusion
  91.3 2.8 %fusion.50 = f32[8,512,128]{1,2,0:T(8,128)} fusion(bf16[8,512,512]{2,1,0:T(8,128)(2,1)S(1)} %select_convert_fusion, bf16[512,1024]{1,0:T(8,128)(2,1)S(1)} %copy-done.9), kind=kOutput, calls=%fused_computation.69 | convolution fusion | flops 536870912 | bytes 7340032 | tf_op jit(solution)/shard_map/hts,shd->thd/dot_general | solution.py:99
  94.1 2.1 %fusion.86 = f32[8,512,128]{1,2,0:T(8,128)} fusion(bf16[512,8,128]{0,2,1:T(8,128)(2,1)S(1)} %bitcast.103, bf16[8,512,512]{2,1,0:T(8,128)(2,1)S(1)} %select_convert_fusion), kind=kOutput, calls=%fused_computation.134 | convolution fusion | flops 536870912 | bytes 7340032 | tf_op jit(solution)/shard_map/hts,thd->shd/dot_general | solution.py:101
  96.2 2.4 %copy.35 = bf16[512,1024]{1,0:T(8,128)(2,1)} copy(bf16[512,1024]{0,1:T(8,128)(2,1)} %bitcast.113) | data formatting | bytes 2097152
  98.5 3.8 %fusion.21 = bf16[512,8,128]{0,2,1:T(8,128)(2,1)} fusion(f32[8,512,128]{1,2,0:T(8,128)} %fusion.50, bf16[512,8,128]{0,2,1:T(8,128)(2,1)S(1)} %bitcast.107, f32[512]{0:T(512)S(1)} %multiply_rsqrt_fusion, f32[2,8,128,128]{3,2,1,0:T(8,128)} %copy-done.3), kind=kOutput, calls=%fused_computation.28 | convolution fusion | flops 806879232 | bytes 4720640 | tf_op jit(solution)/shard_map/thj,hij->thi/dot_general | solution.py:100
  102.3 2.4 %copy.33 = bf16[512,1024]{1,0:T(8,128)(2,1)} copy(bf16[512,1024]{0,1:T(8,128)(2,1)} %bitcast.119) | data formatting | bytes 2097152
  104.6 3.6 %fusion.20 = bf16[512,8,128]{0,2,1:T(8,128)(2,1)} fusion(f32[8,512,128]{1,2,0:T(8,128)} %fusion.86, f32[2,8,128,128]{3,2,1,0:T(8,128)S(1)} %copy-done.4, bf16[512,1024]{1,0:T(8,128)(2,1)S(1)} %copy-done), kind=kOutput, calls=%fused_computation.26 | convolution fusion | flops 806354944 | bytes 4718592 | tf_op jit(solution)/shard_map/shj,hij->shi/dot_general | solution.py:102
  108.2 2.3 %copy.34 = bf16[512,1024]{1,0:T(8,128)(2,1)} copy(bf16[512,1024]{0,1:T(8,128)(2,1)} %bitcast.120) | data formatting | bytes 2097152
  110.5 1.5 collective-permute-start.16
  112.5 1.5 collective-permute-start.13
  114.6 5.2 %add_convert_fusion = bf16[2048,1024]{0,1:T(8,128)(2,1)S(1)} fusion(bf16[2048,1024]{0,1:T(8,128)(2,1)} %collective-permute-done.18, bf16[512,1024]{0,1:T(8,128)(2,1)S(1)} %bitcast.114, bf16[512,512]{1,0:T(8,128)(2,1)} %get-tuple-element.31, bf16[512,512]{1,0:T(8,128)(2,1)} %get-tuple-element.32, bf16[512,512]{1,0:T(8,128)(2,1)} %get-tuple-element.33, ...), kind=kOutput, calls=%fused_computation | convolution fusion | flops 2168455168 | bytes 11534336 | tf_op jit(solution)/shard_map/dot_general | solution.py:141
  119.8 1.4 fusion.85
  121.2 1.5 collective-permute-start.20
  122.7 2.8 %collective-permute-done.16 = bf16[512,512]{0,1:T(8,128)(2,1)S(1)} collective-permute-done((bf16[512,512]{0,1:T(8,128)(2,1)}, bf16[512,512]{0,1:T(8,128)(2,1)S(1)}, u32[]{:S(2)}, u32[]{:S(2)}) %collective-permute-start.16) | collective-permute-done | bytes 524320 | tf_op jit(solution)/shard_map/ppermute | solution.py:13
  125.5 1.9 fusion.28
  127.5 2.6 %collective-permute-start.17 = (bf16[512,512]{0,1:T(8,128)(2,1)S(1)}, bf16[512,512]{0,1:T(8,128)(2,1)S(1)}, u32[]{:S(2)}, u32[]{:S(2)}) collective-permute-start(bf16[512,512]{0,1:T(8,128)(2,1)S(1)} %fusion.28), channel_id=1, source_target_pairs={{0,2},{1,3},{2,0},{3,1},{4,6},{5,7},{6,4},{7,5},{8,10},{9,11},{10,... | collective-permute-start | bytes 1572872 | tf_op jit(solution)/shard_map/ppermute | solution.py:13
  130.1 29.1 %collective-permute-done.13 = bf16[512,512]{0,1:T(8,128)(2,1)S(1)} collective-permute-done((bf16[512,512]{0,1:T(8,128)(2,1)}, bf16[512,512]{0,1:T(8,128)(2,1)S(1)}, u32[]{:S(2)}, u32[]{:S(2)}) %collective-permute-start.13) | collective-permute-done | bytes 524320 | tf_op jit(solution)/shard_map/ppermute | solution.py:13
  159.2 1.5 collective-permute-start.23
  160.7 1.9 fusion.35
  162.7 1.8 collective-permute-start.14
  164.5 0.9 add_convert_fusion.2
  165.5 5.8 %collective-permute-done.23 = bf16[512,512]{0,1:T(8,128)(2,1)S(1)} collective-permute-done((bf16[512,512]{0,1:T(8,128)(2,1)S(1)}, bf16[512,512]{0,1:T(8,128)(2,1)S(1)}, u32[]{:S(2)}, u32[]{:S(2)}) %collective-permute-start.23) | collective-permute-done | bytes 524320 | tf_op jit(solution)/shard_map/ppermute | solution.py:13
  171.2 1.5 collective-permute-start.19
  172.7 0.9 add_convert_fusion.1
  173.6 1.5 collective-permute-start.22
  175.7 0.6 collective-permute-start.24
  176.2 2.0 fusion.32
  178.2 15.8 %collective-permute-done.14 = bf16[512,512]{0,1:T(8,128)(2,1)S(1)} collective-permute-done((bf16[512,512]{0,1:T(8,128)(2,1)S(1)}, bf16[512,512]{0,1:T(8,128)(2,1)S(1)}, u32[]{:S(2)}, u32[]{:S(2)}) %collective-permute-start.14) | collective-permute-done | bytes 524320 | tf_op jit(solution)/shard_map/ppermute | solution.py:13
  194.0 2.0 fusion.39
  196.0 1.3 copy.32
  197.4 2.0 convert_add_fusion.3
  199.5 1.8 copy.36
  (75 shorter events, 3.8 us)
Async XLA Ops:
  0.6 3.1 %copy-start = (bf16[512,1024]{1,0:T(8,128)(2,1)S(1)}, bf16[512,1024]{1,0:T(8,128)(2,1)}, u32[]{:S(2)}) copy-start(bf16[512,1024]{1,0:T(8,128)(2,1)} %param.9) | copy-start | bytes 3145732
  5.5 3.1 %copy-start.5 = (f32[1,8,128,128]{3,2,1,0:T(8,128)}, f32[1,8,128,128]{3,2,1,0:T(8,128)S(1)}, u32[]{:S(2)}) copy-start(f32[1,8,128,128]{3,2,1,0:T(8,128)S(1)} %convolution_bitcast_fusion) | copy-start | bytes 1572868
  6.9 0.8 copy-start.1
  8.6 9.5 %collective-permute-start = (bf16[2,8,128,128]{3,2,1,0:T(8,128)(2,1)}, bf16[2,8,128,128]{3,2,1,0:T(8,128)(2,1)}, u32[]{:S(2)}, u32[]{:S(2)}) collective-permute-start(bf16[2,8,128,128]{3,2,1,0:T(8,128)(2,1)} %fusion.64), channel_id=1, source_target_pairs={{0,4},{4,0},{8,12},{12,8},{16,20},{20,16},{24,28},{28,24},{1,5},{5... | collective-permute-start | bytes 1572872 | tf_op jit(solution)/shard_map/ppermute | solution.py:13
  9.1 47.3 %collective-permute-start.3 = (bf16[512,1024]{1,0:T(8,128)(2,1)}, bf16[512,1024]{1,0:T(8,128)(2,1)}, u32[]{:S(2)}, u32[]{:S(2)}) collective-permute-start(bf16[512,1024]{1,0:T(8,128)(2,1)} %param.11), channel_id=1, source_target_pairs={{0,4},{4,0},{8,12},{12,8},{16,20},{20,16},{24,28},{28,24},{1,5},{5... | collective-permute-start | bytes 3145736 | tf_op jit(solution)/shard_map/ppermute | solution.py:13
  9.1 44.0 %collective-permute-start.4 = (bf16[512,1024]{1,0:T(8,128)(2,1)}, bf16[512,1024]{1,0:T(8,128)(2,1)}, u32[]{:S(2)}, u32[]{:S(2)}) collective-permute-start(bf16[512,1024]{1,0:T(8,128)(2,1)} %param.11), channel_id=1, source_target_pairs={{0,8},{4,12},{8,0},{12,4},{16,24},{20,28},{24,16},{28,20},{1,9},{5... | collective-permute-start | bytes 3145736 | tf_op jit(solution)/shard_map/ppermute | solution.py:13
  12.1 38.4 %collective-permute-start.6 = (bf16[512,1024]{1,0:T(8,128)(2,1)}, bf16[512,1024]{1,0:T(8,128)(2,1)}, u32[]{:S(2)}, u32[]{:S(2)}) collective-permute-start(bf16[512,1024]{1,0:T(8,128)(2,1)} %param.11), channel_id=1, source_target_pairs={{0,16},{4,20},{8,24},{12,28},{16,0},{20,4},{24,8},{28,12},{1,17},{... | collective-permute-start | bytes 3145736 | tf_op jit(solution)/shard_map/ppermute | solution.py:13
  13.7 4.4 %copy-start.2 = (f32[1,8,128,128]{3,2,1,0:T(8,128)S(1)}, f32[1,8,128,128]{3,2,1,0:T(8,128)}, u32[]{:S(2)}) copy-start(f32[1,8,128,128]{3,2,1,0:T(8,128)} %copy-done.1) | copy-start | bytes 1572868
  13.7 4.4 %copy-start.6 = (f32[1,8,128,128]{3,2,1,0:T(8,128)S(1)}, f32[1,8,128,128]{3,2,1,0:T(8,128)}, u32[]{:S(2)}) copy-start(f32[1,8,128,128]{3,2,1,0:T(8,128)} %copy-done.5) | copy-start | bytes 1572868
  20.1 26.9 %collective-permute-start.1 = (bf16[2,8,128,128]{3,2,1,0:T(8,128)(2,1)}, bf16[2,8,128,128]{3,2,1,0:T(8,128)(2,1)}, u32[]{:S(2)}, u32[]{:S(2)}) collective-permute-start(bf16[2,8,128,128]{3,2,1,0:T(8,128)(2,1)} %fusion.73), channel_id=1, source_target_pairs={{0,8},{4,12},{8,0},{12,4},{16,24},{20,28},{24,16},{28,20},{1,9},{5... | collective-permute-start | bytes 1572872 | tf_op jit(solution)/shard_map/ppermute | solution.py:13
  48.7 24.6 %collective-permute-start.2 = (bf16[2,8,128,128]{3,2,1,0:T(8,128)(2,1)S(1)}, bf16[2,8,128,128]{3,2,1,0:T(8,128)(2,1)S(1)}, u32[]{:S(2)}, u32[]{:S(2)}) collective-permute-start(bf16[2,8,128,128]{3,2,1,0:T(8,128)(2,1)S(1)} %fusion.45), channel_id=1, source_target_pairs={{0,16},{4,20},{8,24},{12,28},{16,0},{20,4},{24,8},{28,12},{1,17},{... | collective-permute-start | bytes 1572872 | tf_op jit(solution)/shard_map/ppermute | solution.py:13
  51.6 12.8 %collective-permute-start.8 = (bf16[256,1024]{1,0:T(8,128)(2,1)S(1)}, bf16[256,1024]{1,0:T(8,128)(2,1)S(1)}, u32[]{:S(2)}, u32[]{:S(2)}) collective-permute-start(bf16[256,1024]{1,0:T(8,128)(2,1)S(1)} %slice.72), channel_id=1, source_target_pairs={{0,8},{4,12},{8,0},{12,4},{16,24},{20,28},{24,16},{28,20},{1,9},{5... | collective-permute-start | bytes 1572872 | tf_op jit(solution)/shard_map/ppermute | solution.py:13
  54.2 19.0 %collective-permute-start.9 = (bf16[256,1024]{1,0:T(8,128)(2,1)S(1)}, bf16[256,1024]{1,0:T(8,128)(2,1)S(1)}, u32[]{:S(2)}, u32[]{:S(2)}) collective-permute-start(bf16[256,1024]{1,0:T(8,128)(2,1)S(1)} %slice.73), channel_id=1, source_target_pairs={{0,16},{4,20},{8,24},{12,28},{16,0},{20,4},{24,8},{28,12},{1,17},{... | collective-permute-start | bytes 1572872 | tf_op jit(solution)/shard_map/ppermute | solution.py:13
  54.9 19.9 %copy-start.8 = (bf16[512,1024]{1,0:T(8,128)(2,1)S(1)}, bf16[512,1024]{1,0:T(8,128)(2,1)}, u32[]{:S(2)}) copy-start(bf16[512,1024]{1,0:T(8,128)(2,1)} %param.8) | copy-start | bytes 3145732
  54.9 19.9 %copy-start.12 = (f32[8,512,128]{1,2,0:T(8,128)S(1)}, f32[8,512,128]{1,2,0:T(8,128)}, u32[]{:S(2)}) copy-start(f32[8,512,128]{1,2,0:T(8,128)} %fusion) | copy-start | bytes 6291460
  54.9 21.1 %collective-permute-start.5 = (bf16[512,1024]{1,0:T(8,128)(2,1)}, bf16[512,1024]{1,0:T(8,128)(2,1)S(1)}, u32[]{:S(2)}, u32[]{:S(2)}) collective-permute-start(bf16[512,1024]{1,0:T(8,128)(2,1)} %collective-permute-done.4), channel_id=1, source_target_pairs={{0,4},{4,0},{8,12},{12,8},{16,20},{20,16},{24,28},{28,24},{1,5},{5... | collective-permute-start | bytes 3145736 | tf_op jit(solution)/shard_map/ppermute | solution.py:13
  56.4 21.3 %collective-permute-start.7 = (bf16[512,1024]{1,0:T(8,128)(2,1)}, bf16[512,1024]{1,0:T(8,128)(2,1)S(1)}, u32[]{:S(2)}, u32[]{:S(2)}) collective-permute-start(bf16[512,1024]{1,0:T(8,128)(2,1)} %collective-permute-done.6), channel_id=1, source_target_pairs={{0,4},{4,0},{8,12},{12,8},{16,20},{20,16},{24,28},{28,24},{1,5},{5... | collective-permute-start | bytes 3145736 | tf_op jit(solution)/shard_map/ppermute | solution.py:13
  64.3 13.5 %collective-permute-start.10 = (bf16[256,1024]{1,0:T(8,128)(2,1)S(1)}, bf16[256,1024]{1,0:T(8,128)(2,1)S(1)}, u32[]{:S(2)}, u32[]{:S(2)}) collective-permute-start(bf16[256,1024]{1,0:T(8,128)(2,1)S(1)} %collective-permute-done.8), channel_id=1, source_target_pairs={{0,4},{4,0},{8,12},{12,8},{16,20},{20,16},{24,28},{28,24},{1,5},{5... | collective-permute-start | bytes 1572872 | tf_op jit(solution)/shard_map/ppermute | solution.py:13
  73.2 4.7 %collective-permute-start.11 = (bf16[256,1024]{1,0:T(8,128)(2,1)S(1)}, bf16[256,1024]{1,0:T(8,128)(2,1)S(1)}, u32[]{:S(2)}, u32[]{:S(2)}) collective-permute-start(bf16[256,1024]{1,0:T(8,128)(2,1)S(1)} %collective-permute-done.9), channel_id=1, source_target_pairs={{0,4},{4,0},{8,12},{12,8},{16,20},{20,16},{24,28},{28,24},{1,5},{5... | collective-permute-start | bytes 1572872 | tf_op jit(solution)/shard_map/ppermute | solution.py:13
  74.8 2.9 %copy-start.3 = (f32[2,8,128,128]{3,2,1,0:T(8,128)}, f32[2,8,128,128]{3,2,1,0:T(8,128)S(1)}, u32[]{:S(2)}) copy-start(f32[2,8,128,128]{3,2,1,0:T(8,128)S(1)} %fusion.44) | copy-start | bytes 3145732
  76.0 8.7 %copy-start.10 = (bf16[512,8,128]{0,2,1:T(8,128)(2,1)}, bf16[512,8,128]{0,2,1:T(8,128)(2,1)S(1)}, u32[]{:S(2)}) copy-start(bf16[512,8,128]{0,2,1:T(8,128)(2,1)S(1)} %fusion.22) | copy-start | bytes 3145732
  78.0 5.2 %copy-start.17 = (bf16[4096,1024]{1,0:T(8,128)(2,1)}, bf16[4096,1024]{1,0:T(8,128)(2,1)S(1)}, u32[]{:S(2)}) copy-start(bf16[4096,1024]{1,0:T(8,128)(2,1)S(1)} %constant_dynamic-update-slice_fusion) | copy-start | bytes 25165828
  81.6 3.0 %copy-start.13 = (bf16[512,512]{1,0:T(8,128)(2,1)S(1)}, bf16[512,512]{1,0:T(8,128)(2,1)}, u32[]{:S(2)}) copy-start(bf16[512,512]{1,0:T(8,128)(2,1)} %get-tuple-element.29) | copy-start | bytes 1572868
  81.6 3.0 %copy-start.14 = (bf16[512,512]{1,0:T(8,128)(2,1)S(1)}, bf16[512,512]{1,0:T(8,128)(2,1)}, u32[]{:S(2)}) copy-start(bf16[512,512]{1,0:T(8,128)(2,1)} %get-tuple-element.30) | copy-start | bytes 1572868
  81.6 3.0 %copy-start.15 = (bf16[512,512]{1,0:T(8,128)(2,1)S(1)}, bf16[512,512]{1,0:T(8,128)(2,1)}, u32[]{:S(2)}) copy-start(bf16[512,512]{1,0:T(8,128)(2,1)} %get-tuple-element.34) | copy-start | bytes 1572868
  81.6 3.0 %copy-start.16 = (bf16[512,512]{1,0:T(8,128)(2,1)S(1)}, bf16[512,512]{1,0:T(8,128)(2,1)}, u32[]{:S(2)}) copy-start(bf16[512,512]{1,0:T(8,128)(2,1)} %get-tuple-element.35) | copy-start | bytes 1572868
  89.0 25.6 %collective-permute-start.18 = (bf16[2048,1024]{0,1:T(8,128)(2,1)}, bf16[2048,1024]{0,1:T(8,128)(2,1)}, u32[]{:S(2)}, u32[]{:S(2)}) collective-permute-start(bf16[2048,1024]{0,1:T(8,128)(2,1)} %multiply_convert_fusion), channel_id=1, source_target_pairs={{0,4},{4,0},{8,12},{12,8},{16,20},{20,16},{24,28},{28,24},{1,5},{5... | collective-permute-start | bytes 12582920 | tf_op jit(solution)/shard_map/ppermute | solution.py:13
  89.5 1.7 copy-start.9
  96.2 8.5 %copy-start.4 = (f32[2,8,128,128]{3,2,1,0:T(8,128)S(1)}, f32[2,8,128,128]{3,2,1,0:T(8,128)}, u32[]{:S(2)}) copy-start(f32[2,8,128,128]{3,2,1,0:T(8,128)} %copy-done.3) | copy-start | bytes 3145732
  102.3 12.3 %copy-start.11 = (bf16[512,8,128]{0,2,1:T(8,128)(2,1)S(1)}, bf16[512,8,128]{0,2,1:T(8,128)(2,1)}, u32[]{:S(2)}) copy-start(bf16[512,8,128]{0,2,1:T(8,128)(2,1)} %copy-done.10) | copy-start | bytes 3145732
  110.5 15.0 %collective-permute-start.16 = (bf16[512,512]{0,1:T(8,128)(2,1)}, bf16[512,512]{0,1:T(8,128)(2,1)S(1)}, u32[]{:S(2)}, u32[]{:S(2)}) collective-permute-start(bf16[512,512]{0,1:T(8,128)(2,1)} %convolution_convert_fusion.3), channel_id=1, source_target_pairs={{0,1},{1,0},{2,3},{3,2},{4,5},{5,4},{6,7},{7,6},{8,9},{9,8},{10,11... | collective-permute-start | bytes 1572872 | tf_op jit(solution)/shard_map/ppermute | solution.py:13
  112.1 61.6 %collective-permute-start.15 = (bf16[512,512]{0,1:T(8,128)(2,1)}, bf16[512,512]{0,1:T(8,128)(2,1)S(1)}, u32[]{:S(2)}, u32[]{:S(2)}) collective-permute-start(bf16[512,512]{0,1:T(8,128)(2,1)} %convolution_convert_fusion.5), channel_id=1, source_target_pairs={{0,1},{1,0},{2,3},{3,2},{4,5},{5,4},{6,7},{7,6},{8,9},{9,8},{10,11... | collective-permute-start | bytes 1572872 | tf_op jit(solution)/shard_map/ppermute | solution.py:13
  112.5 46.7 %collective-permute-start.13 = (bf16[512,512]{0,1:T(8,128)(2,1)}, bf16[512,512]{0,1:T(8,128)(2,1)S(1)}, u32[]{:S(2)}, u32[]{:S(2)}) collective-permute-start(bf16[512,512]{0,1:T(8,128)(2,1)} %convolution_convert_fusion.4), channel_id=1, source_target_pairs={{0,1},{1,0},{2,3},{3,2},{4,5},{5,4},{6,7},{7,6},{8,9},{9,8},{10,11... | collective-permute-start | bytes 1572872 | tf_op jit(solution)/shard_map/ppermute | solution.py:13
  114.1 61.1 %collective-permute-start.12 = (bf16[512,512]{0,1:T(8,128)(2,1)}, bf16[512,512]{0,1:T(8,128)(2,1)S(1)}, u32[]{:S(2)}, u32[]{:S(2)}) collective-permute-start(bf16[512,512]{0,1:T(8,128)(2,1)} %convolution_convert_fusion.6), channel_id=1, source_target_pairs={{0,1},{1,0},{2,3},{3,2},{4,5},{5,4},{6,7},{7,6},{8,9},{9,8},{10,11... | collective-permute-start | bytes 1572872 | tf_op jit(solution)/shard_map/ppermute | solution.py:13
  119.8 7.7 %copy-start.7 = (bf16[2048,1024]{0,1:T(8,128)(2,1)}, bf16[2048,1024]{0,1:T(8,128)(2,1)S(1)}, u32[]{:S(2)}) copy-start(bf16[2048,1024]{0,1:T(8,128)(2,1)S(1)} %add_convert_fusion) | copy-start | bytes 12582916
  121.2 41.4 %collective-permute-start.20 = (bf16[512,512]{0,1:T(8,128)(2,1)S(1)}, bf16[512,512]{0,1:T(8,128)(2,1)S(1)}, u32[]{:S(2)}, u32[]{:S(2)}) collective-permute-start(bf16[512,512]{0,1:T(8,128)(2,1)S(1)} %get-tuple-element.26), channel_id=1, source_target_pairs={{0,8},{4,12},{8,0},{12,4},{16,24},{20,28},{24,16},{28,20},{1,9},{5... | collective-permute-start | bytes 1572872 | tf_op jit(solution)/shard_map/ppermute | solution.py:13
  127.5 48.2 %collective-permute-start.17 = (bf16[512,512]{0,1:T(8,128)(2,1)S(1)}, bf16[512,512]{0,1:T(8,128)(2,1)S(1)}, u32[]{:S(2)}, u32[]{:S(2)}) collective-permute-start(bf16[512,512]{0,1:T(8,128)(2,1)S(1)} %fusion.28), channel_id=1, source_target_pairs={{0,2},{1,3},{2,0},{3,1},{4,6},{5,7},{6,4},{7,5},{8,10},{9,11},{10,... | collective-permute-start | bytes 1572872 | tf_op jit(solution)/shard_map/ppermute | solution.py:13
  159.2 12.0 %collective-permute-start.23 = (bf16[512,512]{0,1:T(8,128)(2,1)S(1)}, bf16[512,512]{0,1:T(8,128)(2,1)S(1)}, u32[]{:S(2)}, u32[]{:S(2)}) collective-permute-start(bf16[512,512]{0,1:T(8,128)(2,1)S(1)} %get-tuple-element.23), channel_id=1, source_target_pairs={{0,16},{4,20},{8,24},{12,28},{16,0},{20,4},{24,8},{28,12},{1,17},{... | collective-permute-start | bytes 1572872 | tf_op jit(solution)/shard_map/ppermute | solution.py:13
  162.7 31.3 %collective-permute-start.14 = (bf16[512,512]{0,1:T(8,128)(2,1)S(1)}, bf16[512,512]{0,1:T(8,128)(2,1)S(1)}, u32[]{:S(2)}, u32[]{:S(2)}) collective-permute-start(bf16[512,512]{0,1:T(8,128)(2,1)S(1)} %fusion.35), channel_id=1, source_target_pairs={{0,2},{1,3},{2,0},{3,1},{4,6},{5,7},{6,4},{7,5},{8,10},{9,11},{10,... | collective-permute-start | bytes 1572872 | tf_op jit(solution)/shard_map/ppermute | solution.py:13
  171.2 26.1 %collective-permute-start.19 = (bf16[512,512]{0,1:T(8,128)(2,1)}, bf16[512,512]{0,1:T(8,128)(2,1)S(1)}, u32[]{:S(2)}, u32[]{:S(2)}) collective-permute-start(bf16[512,512]{0,1:T(8,128)(2,1)} %get-tuple-element.22), channel_id=1, source_target_pairs={{0,8},{4,12},{8,0},{12,4},{16,24},{20,28},{24,16},{28,20},{1,9},{5... | collective-permute-start | bytes 1572872 | tf_op jit(solution)/shard_map/ppermute | solution.py:13
  173.6 23.7 %collective-permute-start.22 = (bf16[512,512]{0,1:T(8,128)(2,1)}, bf16[512,512]{0,1:T(8,128)(2,1)S(1)}, u32[]{:S(2)}, u32[]{:S(2)}) collective-permute-start(bf16[512,512]{0,1:T(8,128)(2,1)} %get-tuple-element.25), channel_id=1, source_target_pairs={{0,16},{4,20},{8,24},{12,28},{16,0},{20,4},{24,8},{28,12},{1,17},{... | collective-permute-start | bytes 1572872 | tf_op jit(solution)/shard_map/ppermute | solution.py:13
  175.2 22.2 %collective-permute-start.21 = (bf16[512,512]{0,1:T(8,128)(2,1)}, bf16[512,512]{0,1:T(8,128)(2,1)}, u32[]{:S(2)}, u32[]{:S(2)}) collective-permute-start(bf16[512,512]{0,1:T(8,128)(2,1)} %add_convert_fusion.2), channel_id=1, source_target_pairs={{0,16},{4,20},{8,24},{12,28},{16,0},{20,4},{24,8},{28,12},{1,17},{... | collective-permute-start | bytes 1572872 | tf_op jit(solution)/shard_map/ppermute | solution.py:13
  175.7 21.7 %collective-permute-start.24 = (bf16[512,512]{0,1:T(8,128)(2,1)}, bf16[512,512]{0,1:T(8,128)(2,1)}, u32[]{:S(2)}, u32[]{:S(2)}) collective-permute-start(bf16[512,512]{0,1:T(8,128)(2,1)} %add_convert_fusion.1), channel_id=1, source_target_pairs={{0,8},{4,12},{8,0},{12,4},{16,24},{20,28},{24,16},{28,20},{1,9},{5... | collective-permute-start | bytes 1572872 | tf_op jit(solution)/shard_map/ppermute | solution.py:13
